TPU v7x, 32 devices: a whole 2x2x4 slice. The times are simulated.
32 devices in a mesh: group: 4 (over y, x), member: 8 (over z, core).
Axes of the slice: x: 2, y: 2, z: 4, core: 2. Of those that a mesh axis runs over, the one named last changes fastest.
Arguments:
- activations: bfloat16 [4, 1024, 2048], P('group', 'member'), may hold values from -6 to 6
- lengths: int32 [4, 8], P('group'), may hold values from 1 to 128, 576 in all within a row
- assignment: int32 [4, 8], P('group'), may hold values from 0 to 7, each once within a row
- owners: int32 [4], replicated, may hold values from 0 to 3
- prefix_cache: bfloat16 [4, 8192, 256], P('group', 'member'), may hold values from -244 to 244
- first_gain: float32 [2048], replicated, may hold values from 0.1 to 1.9
- first_bias: float32 [2048], replicated, may hold values from -3 to 3
- query_weight: bfloat16 [2048, 2048], replicated, may hold values from -0.125 to 0.125
- keyval_weight: bfloat16 [2048, 256], replicated, may hold values from -0.4375 to 0.4375
- output_weight: bfloat16 [2048, 2048], replicated, may hold values from -0.125 to 0.125
- second_gain: float32 [2048], replicated, may hold values from 0.1 to 1.9
- second_bias: float32 [2048], replicated, may hold values from -3 to 3
- expand_weight: bfloat16 [2048, 8192], P(None, 'member'), may hold values from -0.125 to 0.125
- contract_weight: bfloat16 [8192, 2048], P('member'), may hold values from -0.0625 to 0.0625
Outputs:
- layer_output: bfloat16 [4, 1024, 2048], P('group', 'member')
Inputs may be any that keep to these rules, and one draw needn't show every extreme that they name: Each row of lengths sums to 576 and its longest entry is 128. Each row of assignment names every request of its group once. `owners`: several groups may attend the same cache slot.
All inputs are finite; a program needn't handle non-finite values.
Results may differ from a plain program's by a relative error of at most 0.011.
The roundings to bfloat16 on the way count: a program that leaves them out, or rounds other values in their place, can miss the bound.
Values may be sent and summed in bfloat16 or wider, within the bound.
No kernel may reach another device: no remote copies, remote signals or barrier semaphores. Data moves between devices by JAX's collectives and lax.ppermute only.
A program may use at most 128 MiB of HBM per device.

v0:
```python
import math
import jax
import jax.numpy as jnp
from jax import lax
from jax.sharding import PartitionSpec as P

EPSILON = 1e-05
NEGATIVE = -1e30


def layer_norm(values, gain, bias):
    average = jnp.mean(values, axis=-1, keepdims=True)
    centered = values - average
    spread = jnp.mean(centered * centered, axis=-1, keepdims=True)
    return centered * lax.rsqrt(spread + EPSILON) * gain + bias


def pick_value(table, wanted):
    slots_at = lax.broadcasted_iota(jnp.int32, table.shape, 0)
    return jnp.sum(jnp.where(slots_at == wanted, table, 0))


def own_scores(query_block, own_keys, scaling):
    scores = (
        jnp.einsum("thd,sd->ths", query_block, own_keys, preferred_element_type=jnp.float32)
        * scaling
    )
    block_rows = query_block.shape[0]
    key_rows = own_keys.shape[0]
    row_at = lax.broadcasted_iota(jnp.int32, (block_rows, 1, key_rows), 0)
    column_at = lax.broadcasted_iota(jnp.int32, (block_rows, 1, key_rows), 2)
    return jnp.where(column_at <= row_at, scores, NEGATIVE)


def folded_attention(queries, keys_values, selected):
    row_count, head_count, head_size = queries.shape
    scaling = 1.0 / math.sqrt(head_size)
    own_keys = keys_values[:, :head_size]
    own_values = keys_values[:, head_size:]
    suffix_scores = own_scores(queries, own_keys, scaling)
    highest = jnp.max(suffix_scores, axis=-1)
    suffix_exp = jnp.exp(suffix_scores - highest[..., None])
    denominator = jnp.sum(suffix_exp, axis=-1)
    weighted = jnp.einsum(
        "ths,sd->thd",
        suffix_exp.astype(jnp.bfloat16),
        own_values,
        preferred_element_type=jnp.float32,
    )
    running = (weighted, highest, denominator)
    portion = lax.all_gather(selected, "member", axis=0, tiled=True)
    extent = portion.shape[0]
    stride = math.gcd(extent, 1024)

    def advance(state_now, block_index):
        weighted_now, highest_now, denominator_now = state_now
        key_block = lax.dynamic_slice_in_dim(portion, block_index * stride, stride, 0)
        scores = (
            jnp.einsum(
                "thd,pd->thp", queries, key_block[:, :head_size], preferred_element_type=jnp.float32
            )
            * scaling
        )
        highest_next = jnp.maximum(highest_now, jnp.max(scores, axis=-1))
        rescale = jnp.exp(highest_now - highest_next)
        exponent = jnp.exp(scores - highest_next[..., None])
        denominator_next = denominator_now * rescale + jnp.sum(exponent, axis=-1)
        weighted_next = weighted_now * rescale[..., None] + jnp.einsum(
            "thp,pd->thd",
            exponent.astype(jnp.bfloat16),
            key_block[:, head_size:],
            preferred_element_type=jnp.float32,
        )
        return ((weighted_next, highest_next, denominator_next), None)

    running, _ = lax.scan(advance, running, jnp.arange(extent // stride, dtype=jnp.int32))
    weighted, highest, denominator = running
    return (
        (weighted / denominator[..., None])
        .astype(jnp.bfloat16)
        .reshape(row_count, head_count * head_size)
    )


def shards(
    activations,
    lengths,
    assignment,
    owners,
    prefix_cache,
    first_gain,
    first_bias,
    query_weight,
    keyval_weight,
    output_weight,
    second_gain,
    second_bias,
    expand_weight,
    contract_weight,
):
    group_index = lax.axis_index("group")
    member_index = lax.axis_index("member")
    request = pick_value(assignment[0], member_index)
    length_here = pick_value(lengths[0], request)
    owner_here = pick_value(owners, group_index)
    tokens = activations[0]
    row_count = tokens.shape[0]
    head_size = prefix_cache.shape[2] // 2
    head_count = tokens.shape[1] // head_size
    every_block = lax.all_gather(prefix_cache, "group", axis=0, tiled=True)
    selected = lax.dynamic_index_in_dim(every_block, owner_here, 0, keepdims=False)
    tokens_wide = tokens.astype(jnp.float32)
    normed = layer_norm(tokens_wide, first_gain, first_bias).astype(jnp.bfloat16)
    queries = jnp.dot(normed, query_weight, preferred_element_type=jnp.float32).astype(jnp.bfloat16)
    queries = queries.reshape(row_count, head_count, head_size)
    keys_values = jnp.dot(normed, keyval_weight, preferred_element_type=jnp.float32).astype(
        jnp.bfloat16
    )
    attended = folded_attention(queries, keys_values, selected)
    residual = tokens_wide + jnp.dot(attended, output_weight, preferred_element_type=jnp.float32)
    second = layer_norm(residual, second_gain, second_bias).astype(jnp.bfloat16)
    hidden = jax.nn.gelu(
        jnp.dot(
            lax.all_gather(second, "member", axis=0, tiled=True),
            expand_weight,
            preferred_element_type=jnp.float32,
        ),
        approximate=True,
    ).astype(jnp.bfloat16)
    summed = lax.psum_scatter(
        jnp.dot(hidden, contract_weight, preferred_element_type=jnp.float32).astype(jnp.bfloat16),
        "member",
        scatter_dimension=0,
        tiled=True,
    ).astype(jnp.float32)
    is_live = lax.broadcasted_iota(jnp.int32, (row_count, 1), 0) < length_here
    return jnp.where(is_live, residual + summed, 0.0).astype(jnp.bfloat16)[None]


def solution(mesh):
    return jax.shard_map(
        shards,
        mesh=mesh,
        in_specs=(
            P("group", "member", None),
            P("group", None),
            P("group", None),
            P(),
            P("group", "member", None),
            P(),
            P(),
            P(),
            P(),
            P(),
            P(),
            P(),
            P(None, "member"),
            P("member", None),
        ),
        out_specs=P("group", "member", None),
        check_vma=False,
    )
```

profile of v0, /device:TPU:0, one launch (start us, length us, event | category | flops | bytes accessed | tf_op | source)
XLA Modules:
  0.0 286.6 jit_solution(2638500522030421383)
XLA Ops:
  10.5 36.7 %all-gather.5.cloned.1.call-done = bf16[4,1024,256]{2,1,0:T(8,128)(2,1)} async-done(((bf16[1,1024,256]{2,1,0:T(8,128)(2,1)}), bf16[4,1024,256]{2,1,0:T(8,128)(2,1)}) %all-gather.5.cloned.1.call-update) | async-done | bytes 2097168 | tf_op jit(solution)/shard_map/all_gather | solution.py:110
  51.8 5.0 %fusion.30 = bf16[16,16,8,128]{3,2,1,0:T(8,128)(2,1)S(1)} fusion(bf16[2048,2048]{1,0:T(8,128)(2,1)} %param.23, bf16[1,128,2048]{2,1,0:T(8,128)(2,1)} %param.16, f32[2048]{0:T(1024)} %param.22, f32[2048]{0:T(1024)} %param.21, f32[128]{0:T(128)S(1)} %add_rsqrt_fusion.1, f32[128]{0:T(128)S(1)} %broadcast_multiply_fusion.1), kind=kOutput, calls=%fused_computation.39 | convolution fusion | flops 1075576832 | bytes 9454592 | tf_op jit(solution)/shard_map/dot_general | solution.py:114
  58.2 38.3 %all-gather.9.cloned.1.call-done = bf16[1,8192,256]{2,1,0:T(8,128)(2,1)} async-done(((bf16[1,1024,256]{2,1,0:T(8,128)(2,1)}), bf16[1,8192,256]{2,1,0:T(8,128)(2,1)}) %all-gather.9.cloned.1.call-update) | async-done | bytes 4194320 | tf_op jit(solution)/shard_map/all_gather | solution.py:51
  96.4 62.7 %while.14 = (s32[]{:T(128)}, f32[128,16,128]{2,0,1:T(8,128)S(1)}, f32[128,16]{0,1:T(8,128)S(1)}, f32[128,16]{0,1:T(8,128)S(1)}, s32[8]{0:T(128)S(1)}, /*index=5*...) while((s32[]{:T(128)}, f32[128,16,128]{2,0,1:T(8,128)S(1)}, ...), condition=%wide.region_10.11_spmd, body=%wide.region_7.10_spmd.sunk | while | flops 1091047424 | bytes 28442832 | solution.py:76
  97.7 2.2 bitcast_reduce_fusion.2
  101.3 2.9 %fusion.69 = f32[128,16,128]{2,0,1:T(8,128)S(1)} fusion(f32[1024,128,16]{1,0,2:T(8,128)S(1)} %get-tuple-element.135, f32[128,16]{0,1:T(8,128)S(1)} %max.4, f32[128,16,128]{2,0,1:T(8,128)S(1)} %get-tuple-element.152, f32[128,16]{0,1:T(8,128)S(1)} %get-tuple-element.137, bf16[8192,256]{1,0:T(8,128)(2,1)} %get-tuple-element.168, s32[]{:T(128)S(6)} %select_n.46, ...), kind=kOutput, calls=%fused_computation.8.clone.1 | convolution fusion | flops 543686656 | bytes 10764296 | tf_op jit(solution)/shard_map/while/body/eval_jaxpr/thp,pd->thd/dot_general | solution.py:68
  105.5 2.2 bitcast_reduce_fusion.2
  109.2 2.9 %fusion.69 = f32[128,16,128]{2,0,1:T(8,128)S(1)} fusion(f32[1024,128,16]{1,0,2:T(8,128)S(1)} %get-tuple-element.135, f32[128,16]{0,1:T(8,128)S(1)} %max.4, f32[128,16,128]{2,0,1:T(8,128)S(1)} %get-tuple-element.152, f32[128,16]{0,1:T(8,128)S(1)} %get-tuple-element.137, bf16[8192,256]{1,0:T(8,128)(2,1)} %get-tuple-element.168, s32[]{:T(128)S(6)} %select_n.46, ...), kind=kOutput, calls=%fused_computation.8.clone.1 | convolution fusion | flops 543686656 | bytes 10764296 | tf_op jit(solution)/shard_map/while/body/eval_jaxpr/thp,pd->thd/dot_general | solution.py:68
  113.4 2.2 bitcast_reduce_fusion.2
  117.0 2.9 %fusion.69 = f32[128,16,128]{2,0,1:T(8,128)S(1)} fusion(f32[1024,128,16]{1,0,2:T(8,128)S(1)} %get-tuple-element.135, f32[128,16]{0,1:T(8,128)S(1)} %max.4, f32[128,16,128]{2,0,1:T(8,128)S(1)} %get-tuple-element.152, f32[128,16]{0,1:T(8,128)S(1)} %get-tuple-element.137, bf16[8192,256]{1,0:T(8,128)(2,1)} %get-tuple-element.168, s32[]{:T(128)S(6)} %select_n.46, ...), kind=kOutput, calls=%fused_computation.8.clone.1 | convolution fusion | flops 543686656 | bytes 10764296 | tf_op jit(solution)/shard_map/while/body/eval_jaxpr/thp,pd->thd/dot_general | solution.py:68
  121.2 2.2 bitcast_reduce_fusion.2
  124.8 2.9 %fusion.69 = f32[128,16,128]{2,0,1:T(8,128)S(1)} fusion(f32[1024,128,16]{1,0,2:T(8,128)S(1)} %get-tuple-element.135, f32[128,16]{0,1:T(8,128)S(1)} %max.4, f32[128,16,128]{2,0,1:T(8,128)S(1)} %get-tuple-element.152, f32[128,16]{0,1:T(8,128)S(1)} %get-tuple-element.137, bf16[8192,256]{1,0:T(8,128)(2,1)} %get-tuple-element.168, s32[]{:T(128)S(6)} %select_n.46, ...), kind=kOutput, calls=%fused_computation.8.clone.1 | convolution fusion | flops 543686656 | bytes 10764296 | tf_op jit(solution)/shard_map/while/body/eval_jaxpr/thp,pd->thd/dot_general | solution.py:68
  129.0 2.2 bitcast_reduce_fusion.2
  132.7 2.9 %fusion.69 = f32[128,16,128]{2,0,1:T(8,128)S(1)} fusion(f32[1024,128,16]{1,0,2:T(8,128)S(1)} %get-tuple-element.135, f32[128,16]{0,1:T(8,128)S(1)} %max.4, f32[128,16,128]{2,0,1:T(8,128)S(1)} %get-tuple-element.152, f32[128,16]{0,1:T(8,128)S(1)} %get-tuple-element.137, bf16[8192,256]{1,0:T(8,128)(2,1)} %get-tuple-element.168, s32[]{:T(128)S(6)} %select_n.46, ...), kind=kOutput, calls=%fused_computation.8.clone.1 | convolution fusion | flops 543686656 | bytes 10764296 | tf_op jit(solution)/shard_map/while/body/eval_jaxpr/thp,pd->thd/dot_general | solution.py:68
  136.9 2.2 bitcast_reduce_fusion.2
  140.5 2.9 %fusion.69 = f32[128,16,128]{2,0,1:T(8,128)S(1)} fusion(f32[1024,128,16]{1,0,2:T(8,128)S(1)} %get-tuple-element.135, f32[128,16]{0,1:T(8,128)S(1)} %max.4, f32[128,16,128]{2,0,1:T(8,128)S(1)} %get-tuple-element.152, f32[128,16]{0,1:T(8,128)S(1)} %get-tuple-element.137, bf16[8192,256]{1,0:T(8,128)(2,1)} %get-tuple-element.168, s32[]{:T(128)S(6)} %select_n.46, ...), kind=kOutput, calls=%fused_computation.8.clone.1 | convolution fusion | flops 543686656 | bytes 10764296 | tf_op jit(solution)/shard_map/while/body/eval_jaxpr/thp,pd->thd/dot_general | solution.py:68
  144.7 2.2 bitcast_reduce_fusion.2
  148.4 2.9 %fusion.69 = f32[128,16,128]{2,0,1:T(8,128)S(1)} fusion(f32[1024,128,16]{1,0,2:T(8,128)S(1)} %get-tuple-element.135, f32[128,16]{0,1:T(8,128)S(1)} %max.4, f32[128,16,128]{2,0,1:T(8,128)S(1)} %get-tuple-element.152, f32[128,16]{0,1:T(8,128)S(1)} %get-tuple-element.137, bf16[8192,256]{1,0:T(8,128)(2,1)} %get-tuple-element.168, s32[]{:T(128)S(6)} %select_n.46, ...), kind=kOutput, calls=%fused_computation.8.clone.1 | convolution fusion | flops 543686656 | bytes 10764296 | tf_op jit(solution)/shard_map/while/body/eval_jaxpr/thp,pd->thd/dot_general | solution.py:68
  152.6 2.2 bitcast_reduce_fusion.2
  156.2 2.9 %fusion.69 = f32[128,16,128]{2,0,1:T(8,128)S(1)} fusion(f32[1024,128,16]{1,0,2:T(8,128)S(1)} %get-tuple-element.135, f32[128,16]{0,1:T(8,128)S(1)} %max.4, f32[128,16,128]{2,0,1:T(8,128)S(1)} %get-tuple-element.152, f32[128,16]{0,1:T(8,128)S(1)} %get-tuple-element.137, bf16[8192,256]{1,0:T(8,128)(2,1)} %get-tuple-element.168, s32[]{:T(128)S(6)} %select_n.46, ...), kind=kOutput, calls=%fused_computation.8.clone.1 | convolution fusion | flops 543686656 | bytes 10764296 | tf_op jit(solution)/shard_map/while/body/eval_jaxpr/thp,pd->thd/dot_general | solution.py:68
  161.9 4.8 %fusion.51 = (f32[128]{0:T(128)S(1)}, f32[128,2048]{1,0:T(8,128)S(1)}) fusion(bf16[128,2048]{0,1:T(8,128)(2,1)S(1)} %bitcast.88, bf16[2048,2048]{1,0:T(8,128)(2,1)} %param.25, bf16[1,128,2048]{2,1,0:T(8,128)(2,1)S(1)} %copy-done.1), kind=kOutput, calls=%fused_computation.76 | convolution fusion | flops 1074528128 | bytes 10486272 | tf_op jit(solution)/shard_map/dot_general | solution.py:120
  168.2 45.8 %all-gather.7.cloned.1.call-done = bf16[1024,2048]{1,0:T(8,128)(2,1)} async-done(((bf16[128,2048]{1,0:T(8,128)(2,1)}), bf16[1024,2048]{1,0:T(8,128)(2,1)}) %all-gather.7.cloned.1.call-update) | async-done | bytes 4194320 | tf_op jit(solution)/shard_map/all_gather | solution.py:124
  214.0 15.1 %convolution_convert_fusion = bf16[1024,2048]{1,0:T(8,128)(2,1)} fusion(bf16[1024,2048]{1,0:T(8,128)(2,1)} %param.29, bf16[1024,2048]{1,0:T(8,128)(2,1)} %all-gather.7.cloned.1.call-done, bf16[2048,1024]{1,0:T(8,128)(2,1)} %param.28), kind=kOutput, calls=%fused_computation.25 | convolution fusion | flops 8601468928 | bytes 16777216 | tf_op jit(solution)/shard_map/dot_general | solution.py:131
  232.2 45.8 %reduce-scatter.2.cloned.1.call-done = bf16[128,2048]{1,0:T(8,128)(2,1)} async-done(((bf16[1024,2048]{1,0:T(8,128)(2,1)}), bf16[128,2048]{1,0:T(8,128)(2,1)}) %reduce-scatter.2.cloned.1.call-update) | async-done | bytes 524304 | tf_op jit(solution)/shard_map/reduce_scatter | solution.py:130
  (87 shorter events, 33.0 us)
Async XLA Ops:
  6.5 50.4 %copy-start = (bf16[2048,256]{1,0:T(8,128)(2,1)S(1)}, bf16[2048,256]{1,0:T(8,128)(2,1)}, u32[]{:S(2)}) copy-start(bf16[2048,256]{1,0:T(8,128)(2,1)} %param.24) | copy-start | bytes 3145732
  6.5 40.7 %all-gather.5.cloned.1.call-start = ((), (), s32[]{:S(2)}) async-start(), calls=%async_computation.1 | async-start | bytes 2621440 | tf_op jit(solution)/shard_map/all_gather | solution.py:110
  7.3 89.2 %all-gather.9.cloned.1.call-start = ((), (), s32[]{:S(2)}) async-start(), calls=%async_computation.4 | async-start | bytes 4718592 | tf_op jit(solution)/shard_map/all_gather | solution.py:51
  49.1 164.9 %all-gather.7.cloned.1.call-start = ((), (), s32[]{:S(2)}) async-start(), calls=%async_computation.2 | async-start | bytes 4718592 | tf_op jit(solution)/shard_map/all_gather | solution.py:124
  51.7 5.2 %copy-start.1 = (bf16[1,128,2048]{2,1,0:T(8,128)(2,1)S(1)}, bf16[1,128,2048]{2,1,0:T(8,128)(2,1)}, u32[]{:S(2)}) copy-start(bf16[1,128,2048]{2,1,0:T(8,128)(2,1)} %param.16) | copy-start | bytes 1572868
  51.7 5.2 %copy-start.4 = (f32[2048]{0:T(1024)S(1)}, f32[2048]{0:T(1024)}, u32[]{:S(2)}) copy-start(f32[2048]{0:T(1024)} %param.22) | copy-start | bytes 24580
  51.8 5.2 %copy-start.5 = (f32[2048]{0:T(1024)S(1)}, f32[2048]{0:T(1024)}, u32[]{:S(2)}) copy-start(f32[2048]{0:T(1024)} %param.21) | copy-start | bytes 24580
  161.8 5.1 %copy-start.2 = (f32[2048]{0:T(1024)S(1)}, f32[2048]{0:T(1024)}, u32[]{:S(2)}) copy-start(f32[2048]{0:T(1024)} %param.27) | copy-start | bytes 24580
  161.9 5.1 %copy-start.3 = (f32[2048]{0:T(1024)S(1)}, f32[2048]{0:T(1024)}, u32[]{:S(2)}) copy-start(f32[2048]{0:T(1024)} %param.26) | copy-start | bytes 24580
  168.0 110.1 %reduce-scatter.2.cloned.1.call-start = ((), (), s32[]{:S(2)}) async-start(), calls=%async_computation.3 | async-start | bytes 4718592 | tf_op jit(solution)/shard_map/reduce_scatter | solution.py:130
  229.1 0.7 copy-start.6
  229.1 1.3 copy-start.7
Sparse Core Ops, SparseCore 0:
  9.2 38.0 all-gather.4
  49.3 47.1 all-gather.8
  168.1 45.8 all-gather.6
  229.3 48.7 reduce-scatter.1
where the time goes:
time: 288 us; the launch traced here: 287 us
  waiting for transfers between devices  167 us (58%)
  matrix products  67.1 us (23%)
  other arithmetic  22.2 us (8%)
  between operations  15.2 us (5%)
  local copies, waits for them, and re-layouts  8.7 us (3%)
  loops' own time  5.68 us (2%)
    reduce_scatter x1, waiting for transfers between devices, shards(): lax.psum_scatter(jnp.dot(hidden, contract_weight, preferred_element_type=...  45.8 us
    all_gather x1, waiting for transfers between devices, shards(): lax.all_gather(second, 'member', axis=0, tiled=True)  45.8 us
    all_gather x1, waiting for transfers between devices, folded_attention(): portion = lax.all_gather(selected, 'member', axis=0, tiled=True)  38.3 us
    all_gather x1, waiting for transfers between devices, shards(): every_block = lax.all_gather(prefix_cache, 'group', axis=0, tiled=True)  36.7 us
    dot_general x8, matrix products, advance(): jnp.einsum('thp,pd->thd', exponent.astype(jnp.bfloat16), key_block[:, hea...  23.5 us
    dot_general x8, matrix products, advance(): jnp.einsum('thd,pd->thp', queries, key_block[:, :head_size], preferred_el...  17.7 us
    dot_general x1, matrix products, shards(): jnp.dot(hidden, contract_weight, preferred_element_type=jnp.float32)  15.1 us
    reduce_sum x8, other arithmetic, advance(): denominator_next = denominator_now * rescale + jnp.sum(exponent, axis=-1)  11 us
  transfers between devices with their start and end apart: 4, of which 4 were waited for; matrix products, arithmetic and copies ran while one was open for 4% of the time, Pallas kernels for 0%

commit v1 on v0

--- a/solution.py
+++ b/solution.py
@@ -6,6 +6,16 @@
 
 EPSILON = 1e-05
 NEGATIVE = -1e30
+
+
+def ring_gather(x, axis, dim):
+    ways, here, step = (lax.axis_size(axis), lax.axis_index(axis), x.shape[dim])
+    shape = [n * ways if d == dim else n for d, n in enumerate(x.shape)]
+    full = lax.dynamic_update_slice_in_dim(jnp.zeros(shape, x.dtype), x, here * step, axis=dim)
+    for far in range(1, ways):
+        x = lax.ppermute(x, axis, [(d, (d + 1) % ways) for d in range(ways)])
+        full = lax.dynamic_update_slice_in_dim(full, x, (here - far) % ways * step, axis=dim)
+    return full
 
 
 def layer_norm(values, gain, bias):
@@ -121,9 +131,7 @@
     second = layer_norm(residual, second_gain, second_bias).astype(jnp.bfloat16)
     hidden = jax.nn.gelu(
         jnp.dot(
-            lax.all_gather(second, "member", axis=0, tiled=True),
-            expand_weight,
-            preferred_element_type=jnp.float32,
+            ring_gather(second, "member", 0), expand_weight, preferred_element_type=jnp.float32
         ),
         approximate=True,
     ).astype(jnp.bfloat16)

time: 288 us -> 344 us (1.19)
  local copies, waits for them, and re-layouts: 8.7 us -> 34.7 us
  waiting for transfers between devices: 167 us -> 185 us
  matrix products: 67.1 us -> 79.4 us
    ppermute x0 -> x7, waiting for transfers between devices: none -> 64.5 us  [ring_gather(): x = lax.ppermute(x, axis, [(d, (d + 1) % ways) for d in range(ways)])]
    all_gather x1 -> x0, waiting for transfers between devices: 45.8 us -> none  [shards(): lax.all_gather(second, 'member', axis=0, tiled=True)]
    while x8 -> x24, local copies, waits for them, and re-layouts: 0.02 us -> 14.4 us
    dot_general x8, matrix products: 23.5 us -> 35.8 us  [advance(): jnp.einsum('thp,pd->thd', exponent.astype(jnp.bfloat16), key_block[:, hea...]
    dynamic_update_slice x0 -> x7, local copies, waits for them, and re-layouts: none -> 9.06 us  [ring_gather(): lax.dynamic_update_slice_in_dim(full, x, (here - far) % ways * step, axis...]
  transfers between devices with their start and end apart: 4 -> 10, of which waited for: 4 -> 10; matrix products, arithmetic and copies ran while one was open for 4% -> 6% of each run, Pallas kernels for 0% -> 0%
where the time goes in v1:
time: 344 us; the launch traced here: 343 us
  waiting for transfers between devices  185 us (54%)
  matrix products  79.4 us (23%)
  local copies, waits for them, and re-layouts  34.7 us (10%)
  other arithmetic  22.4 us (7%)
  between operations  15.4 us (4%)
  loops' own time  5.68 us (2%)
    ppermute x7, waiting for transfers between devices, ring_gather(): x = lax.ppermute(x, axis, [(d, (d + 1) % ways) for d in range(ways)])  64.5 us
    reduce_scatter x1, waiting for transfers between devices, shards(): lax.psum_scatter(jnp.dot(hidden, contract_weight, preferred_element_type=...  45.2 us
    all_gather x1, waiting for transfers between devices, folded_attention(): portion = lax.all_gather(selected, 'member', axis=0, tiled=True)  38.2 us
    all_gather x1, waiting for transfers between devices, shards(): every_block = lax.all_gather(prefix_cache, 'group', axis=0, tiled=True)  36.7 us
    dot_general x8, matrix products, advance(): jnp.einsum('thp,pd->thd', exponent.astype(jnp.bfloat16), key_block[:, hea...  35.8 us
    dot_general x8, matrix products, advance(): jnp.einsum('thd,pd->thp', queries, key_block[:, :head_size], preferred_el...  17.7 us
    dot_general x1, matrix products, shards(): jnp.dot(hidden, contract_weight, preferred_element_type=jnp.float32)  15.1 us
    while x24, local copies, waits for them, and re-layouts  14.4 us
  transfers between devices with their start and end apart: 10, of which 10 were waited for; matrix products, arithmetic and copies ran while one was open for 6% of the time, Pallas kernels for 0%

profile of v1, /device:TPU:0, one launch (start us, length us, event | category | flops | bytes accessed | tf_op | source)
XLA Modules:
  0.0 343.3 jit_solution(2960412460318985349)
XLA Ops:
  10.5 36.7 %all-gather.4.cloned.1.call-done = bf16[4,1024,256]{2,1,0:T(8,128)(2,1)} async-done(((bf16[1,1024,256]{2,1,0:T(8,128)(2,1)}), bf16[4,1024,256]{2,1,0:T(8,128)(2,1)}) %all-gather.4.cloned.1.call-update) | async-done | bytes 2097168 | tf_op jit(solution)/shard_map/all_gather | solution.py:120
  51.8 5.0 %fusion.30 = bf16[16,16,8,128]{3,2,1,0:T(8,128)(2,1)S(1)} fusion(bf16[2048,2048]{1,0:T(8,128)(2,1)} %param.23, bf16[1,128,2048]{2,1,0:T(8,128)(2,1)} %param.16, f32[2048]{0:T(1024)} %param.22, f32[2048]{0:T(1024)} %param.21, f32[128]{0:T(128)S(1)} %add_rsqrt_fusion.1, f32[128]{0:T(128)S(1)} %broadcast_multiply_fusion.1), kind=kOutput, calls=%fused_computation.39 | convolution fusion | flops 1075576832 | bytes 9454592 | tf_op jit(solution)/shard_map/dot_general | solution.py:124
  58.2 38.2 %all-gather.6.cloned.1.call-done = bf16[1,8192,256]{2,1,0:T(8,128)(2,1)} async-done(((bf16[1,1024,256]{2,1,0:T(8,128)(2,1)}), bf16[1,8192,256]{2,1,0:T(8,128)(2,1)}) %all-gather.6.cloned.1.call-update) | async-done | bytes 4194320 | tf_op jit(solution)/shard_map/all_gather | solution.py:61
  96.4 89.6 %while.14 = (s32[]{:T(128)}, f32[128,16,128]{2,0,1:T(8,128)S(1)}, f32[128,16]{0,1:T(8,128)S(1)}, f32[128,16]{0,1:T(8,128)S(1)}, s32[8]{0:T(128)S(1)}, /*index=5*...) while((s32[]{:T(128)}, f32[128,16,128]{2,0,1:T(8,128)S(1)}, ...), condition=%wide.region_10.11_spmd, body=%wide.region_7.10_spmd.sunk | while | flops 1091047424 | bytes 61997284 | solution.py:86
  97.7 2.2 bitcast_reduce_fusion.2
  103.1 4.5 %fusion.69 = f32[128,16,128]{2,0,1:T(8,128)S(1)} fusion(f32[1024,128,16]{1,0,2:T(8,128)} %copy-done.1, f32[128,16]{0,1:T(8,128)S(1)} %max.4, f32[128,16,128]{2,0,1:T(8,128)S(1)} %get-tuple-element.154, f32[128,16]{0,1:T(8,128)S(1)} %get-tuple-element.139, bf16[8192,256]{1,0:T(8,128)(2,1)} %get-tuple-element.170, s32[]{:T(128)S(6)} %select_n.116, ...), kind=kOutput, calls=%fused_computation.8.clone.1 | convolution fusion | flops 543686656 | bytes 10764296 | tf_op jit(solution)/shard_map/while/body/eval_jaxpr/thp,pd->thd/dot_general | solution.py:78
  114.3 4.5 %fusion.69 = f32[128,16,128]{2,0,1:T(8,128)S(1)} fusion(f32[1024,128,16]{1,0,2:T(8,128)} %copy-done.1, f32[128,16]{0,1:T(8,128)S(1)} %max.4, f32[128,16,128]{2,0,1:T(8,128)S(1)} %get-tuple-element.154, f32[128,16]{0,1:T(8,128)S(1)} %get-tuple-element.139, bf16[8192,256]{1,0:T(8,128)(2,1)} %get-tuple-element.170, s32[]{:T(128)S(6)} %select_n.116, ...), kind=kOutput, calls=%fused_computation.8.clone.1 | convolution fusion | flops 543686656 | bytes 10764296 | tf_op jit(solution)/shard_map/while/body/eval_jaxpr/thp,pd->thd/dot_general | solution.py:78
  125.5 4.5 %fusion.69 = f32[128,16,128]{2,0,1:T(8,128)S(1)} fusion(f32[1024,128,16]{1,0,2:T(8,128)} %copy-done.1, f32[128,16]{0,1:T(8,128)S(1)} %max.4, f32[128,16,128]{2,0,1:T(8,128)S(1)} %get-tuple-element.154, f32[128,16]{0,1:T(8,128)S(1)} %get-tuple-element.139, bf16[8192,256]{1,0:T(8,128)(2,1)} %get-tuple-element.170, s32[]{:T(128)S(6)} %select_n.116, ...), kind=kOutput, calls=%fused_computation.8.clone.1 | convolution fusion | flops 543686656 | bytes 10764296 | tf_op jit(solution)/shard_map/while/body/eval_jaxpr/thp,pd->thd/dot_general | solution.py:78
  136.7 4.5 %fusion.69 = f32[128,16,128]{2,0,1:T(8,128)S(1)} fusion(f32[1024,128,16]{1,0,2:T(8,128)} %copy-done.1, f32[128,16]{0,1:T(8,128)S(1)} %max.4, f32[128,16,128]{2,0,1:T(8,128)S(1)} %get-tuple-element.154, f32[128,16]{0,1:T(8,128)S(1)} %get-tuple-element.139, bf16[8192,256]{1,0:T(8,128)(2,1)} %get-tuple-element.170, s32[]{:T(128)S(6)} %select_n.116, ...), kind=kOutput, calls=%fused_computation.8.clone.1 | convolution fusion | flops 543686656 | bytes 10764296 | tf_op jit(solution)/shard_map/while/body/eval_jaxpr/thp,pd->thd/dot_general | solution.py:78
  147.9 4.5 %fusion.69 = f32[128,16,128]{2,0,1:T(8,128)S(1)} fusion(f32[1024,128,16]{1,0,2:T(8,128)} %copy-done.1, f32[128,16]{0,1:T(8,128)S(1)} %max.4, f32[128,16,128]{2,0,1:T(8,128)S(1)} %get-tuple-element.154, f32[128,16]{0,1:T(8,128)S(1)} %get-tuple-element.139, bf16[8192,256]{1,0:T(8,128)(2,1)} %get-tuple-element.170, s32[]{:T(128)S(6)} %select_n.116, ...), kind=kOutput, calls=%fused_computation.8.clone.1 | convolution fusion | flops 543686656 | bytes 10764296 | tf_op jit(solution)/shard_map/while/body/eval_jaxpr/thp,pd->thd/dot_general | solution.py:78
  159.1 4.5 %fusion.69 = f32[128,16,128]{2,0,1:T(8,128)S(1)} fusion(f32[1024,128,16]{1,0,2:T(8,128)} %copy-done.1, f32[128,16]{0,1:T(8,128)S(1)} %max.4, f32[128,16,128]{2,0,1:T(8,128)S(1)} %get-tuple-element.154, f32[128,16]{0,1:T(8,128)S(1)} %get-tuple-element.139, bf16[8192,256]{1,0:T(8,128)(2,1)} %get-tuple-element.170, s32[]{:T(128)S(6)} %select_n.116, ...), kind=kOutput, calls=%fused_computation.8.clone.1 | convolution fusion | flops 543686656 | bytes 10764296 | tf_op jit(solution)/shard_map/while/body/eval_jaxpr/thp,pd->thd/dot_general | solution.py:78
  170.3 4.5 %fusion.69 = f32[128,16,128]{2,0,1:T(8,128)S(1)} fusion(f32[1024,128,16]{1,0,2:T(8,128)} %copy-done.1, f32[128,16]{0,1:T(8,128)S(1)} %max.4, f32[128,16,128]{2,0,1:T(8,128)S(1)} %get-tuple-element.154, f32[128,16]{0,1:T(8,128)S(1)} %get-tuple-element.139, bf16[8192,256]{1,0:T(8,128)(2,1)} %get-tuple-element.170, s32[]{:T(128)S(6)} %select_n.116, ...), kind=kOutput, calls=%fused_computation.8.clone.1 | convolution fusion | flops 543686656 | bytes 10764296 | tf_op jit(solution)/shard_map/while/body/eval_jaxpr/thp,pd->thd/dot_general | solution.py:78
  181.5 4.5 %fusion.69 = f32[128,16,128]{2,0,1:T(8,128)S(1)} fusion(f32[1024,128,16]{1,0,2:T(8,128)} %copy-done.1, f32[128,16]{0,1:T(8,128)S(1)} %max.4, f32[128,16,128]{2,0,1:T(8,128)S(1)} %get-tuple-element.154, f32[128,16]{0,1:T(8,128)S(1)} %get-tuple-element.139, bf16[8192,256]{1,0:T(8,128)(2,1)} %get-tuple-element.170, s32[]{:T(128)S(6)} %select_n.116, ...), kind=kOutput, calls=%fused_computation.8.clone.1 | convolution fusion | flops 543686656 | bytes 10764296 | tf_op jit(solution)/shard_map/while/body/eval_jaxpr/thp,pd->thd/dot_general | solution.py:78
  188.7 4.7 %fusion.51 = (f32[128]{0:T(128)S(1)}, f32[128,2048]{1,0:T(8,128)S(1)}) fusion(bf16[128,2048]{0,1:T(8,128)(2,1)S(1)} %bitcast.88, bf16[2048,2048]{1,0:T(8,128)(2,1)} %param.25, bf16[1,128,2048]{2,1,0:T(8,128)(2,1)S(1)} %copy-done.2), kind=kOutput, calls=%fused_computation.84 | convolution fusion | flops 1074528128 | bytes 10486272 | tf_op jit(solution)/shard_map/dot_general | solution.py:130
  193.8 2.5 broadcast_in_dim.56
  197.6 10.1 %collective-permute-done = bf16[128,2048]{1,0:T(8,128)(2,1)S(1)} collective-permute-done((bf16[128,2048]{1,0:T(8,128)(2,1)S(1)}, bf16[128,2048]{1,0:T(8,128)(2,1)S(1)}, u32[]{:S(2)}, u32[]{:S(2)}) %collective-permute-start) | collective-permute-done | bytes 524320 | tf_op jit(solution)/shard_map/ppermute | solution.py:16
  207.7 10.4 %collective-permute-done.1 = bf16[128,2048]{1,0:T(8,128)(2,1)S(1)} collective-permute-done((bf16[128,2048]{1,0:T(8,128)(2,1)S(1)}, bf16[128,2048]{1,0:T(8,128)(2,1)S(1)}, u32[]{:S(2)}, u32[]{:S(2)}) %collective-permute-start.1) | collective-permute-done | bytes 524320 | tf_op jit(solution)/shard_map/ppermute | solution.py:16
  218.1 10.4 %collective-permute-done.2 = bf16[128,2048]{1,0:T(8,128)(2,1)S(1)} collective-permute-done((bf16[128,2048]{1,0:T(8,128)(2,1)S(1)}, bf16[128,2048]{1,0:T(8,128)(2,1)S(1)}, u32[]{:S(2)}, u32[]{:S(2)}) %collective-permute-start.2) | collective-permute-done | bytes 524320 | tf_op jit(solution)/shard_map/ppermute | solution.py:16
  228.5 10.4 %collective-permute-done.3 = bf16[128,2048]{1,0:T(8,128)(2,1)S(1)} collective-permute-done((bf16[128,2048]{1,0:T(8,128)(2,1)S(1)}, bf16[128,2048]{1,0:T(8,128)(2,1)S(1)}, u32[]{:S(2)}, u32[]{:S(2)}) %collective-permute-start.3) | collective-permute-done | bytes 524320 | tf_op jit(solution)/shard_map/ppermute | solution.py:16
  239.1 10.4 %collective-permute-done.4 = bf16[128,2048]{1,0:T(8,128)(2,1)} collective-permute-done((bf16[128,2048]{1,0:T(8,128)(2,1)S(1)}, bf16[128,2048]{1,0:T(8,128)(2,1)}, u32[]{:S(2)}, u32[]{:S(2)}) %collective-permute-start.4) | collective-permute-done | bytes 524320 | tf_op jit(solution)/shard_map/ppermute | solution.py:16
  254.1 6.0 %collective-permute-done.5 = bf16[128,2048]{1,0:T(8,128)(2,1)S(1)} collective-permute-done((bf16[128,2048]{1,0:T(8,128)(2,1)}, bf16[128,2048]{1,0:T(8,128)(2,1)S(1)}, u32[]{:S(2)}, u32[]{:S(2)}) %collective-permute-start.5) | collective-permute-done | bytes 524320 | tf_op jit(solution)/shard_map/ppermute | solution.py:16
  263.7 6.8 %collective-permute-done.6 = bf16[128,2048]{1,0:T(8,128)(2,1)S(1)} collective-permute-done((bf16[128,2048]{1,0:T(8,128)(2,1)S(1)}, bf16[128,2048]{1,0:T(8,128)(2,1)S(1)}, u32[]{:S(2)}, u32[]{:S(2)}) %collective-permute-start.6) | collective-permute-done | bytes 524320 | tf_op jit(solution)/shard_map/ppermute | solution.py:16
  271.3 15.1 %convolution_convert_fusion = bf16[1024,2048]{1,0:T(8,128)(2,1)} fusion(bf16[1024,2048]{1,0:T(8,128)(2,1)} %param.29, bf16[1024,2048]{1,0:T(8,128)(2,1)} %constant_dynamic-update-slice_fusion, bf16[2048,1024]{1,0:T(8,128)(2,1)} %param.28), kind=kOutput, calls=%fused_computation.25 | convolution fusion | flops 8601468928 | bytes 16777216 | tf_op jit(solution)/shard_map/dot_general | solution.py:139
  289.5 45.2 %reduce-scatter.2.cloned.1.call-done = bf16[128,2048]{1,0:T(8,128)(2,1)} async-done(((bf16[1024,2048]{1,0:T(8,128)(2,1)}), bf16[128,2048]{1,0:T(8,128)(2,1)}) %reduce-scatter.2.cloned.1.call-update) | async-done | bytes 524304 | tf_op jit(solution)/shard_map/reduce_scatter | solution.py:138
  (126 shorter events, 72.2 us)
Async XLA Ops:
  6.5 50.4 %copy-start = (bf16[2048,256]{1,0:T(8,128)(2,1)S(1)}, bf16[2048,256]{1,0:T(8,128)(2,1)}, u32[]{:S(2)}) copy-start(bf16[2048,256]{1,0:T(8,128)(2,1)} %param.24) | copy-start | bytes 3145732
  6.5 40.7 %all-gather.4.cloned.1.call-start = ((), (), s32[]{:S(2)}) async-start(), calls=%async_computation.1 | async-start | bytes 2621440 | tf_op jit(solution)/shard_map/all_gather | solution.py:120
  7.3 89.2 %all-gather.6.cloned.1.call-start = ((), (), s32[]{:S(2)}) async-start(), calls=%async_computation.3 | async-start | bytes 4718592 | tf_op jit(solution)/shard_map/all_gather | solution.py:61
  49.1 285.6 %reduce-scatter.2.cloned.1.call-start = ((), (), s32[]{:S(2)}) async-start(), calls=%async_computation.2 | async-start | bytes 4718592 | tf_op jit(solution)/shard_map/reduce_scatter | solution.py:138
  51.7 5.2 %copy-start.2 = (bf16[1,128,2048]{2,1,0:T(8,128)(2,1)S(1)}, bf16[1,128,2048]{2,1,0:T(8,128)(2,1)}, u32[]{:S(2)}) copy-start(bf16[1,128,2048]{2,1,0:T(8,128)(2,1)} %param.16) | copy-start | bytes 1572868
  51.7 5.2 %copy-start.7 = (f32[2048]{0:T(1024)S(1)}, f32[2048]{0:T(1024)}, u32[]{:S(2)}) copy-start(f32[2048]{0:T(1024)} %param.22) | copy-start | bytes 24580
  51.8 5.2 %copy-start.8 = (f32[2048]{0:T(1024)S(1)}, f32[2048]{0:T(1024)}, u32[]{:S(2)}) copy-start(f32[2048]{0:T(1024)} %param.21) | copy-start | bytes 24580
  99.9 3.2 copy-start.1
  111.1 3.2 copy-start.1
  122.3 3.2 copy-start.1
  133.5 3.2 copy-start.1
  144.7 3.2 copy-start.1
  155.9 3.2 copy-start.1
  167.1 3.2 copy-start.1
  178.3 3.2 copy-start.1
  197.3 10.4 %collective-permute-start = (bf16[128,2048]{1,0:T(8,128)(2,1)S(1)}, bf16[128,2048]{1,0:T(8,128)(2,1)S(1)}, u32[]{:S(2)}, u32[]{:S(2)}) collective-permute-start(bf16[128,2048]{1,0:T(8,128)(2,1)S(1)} %get-tuple-element.83), channel_id=1, source_target_pairs={{0,1},{1,2},{2,3},{3,4},{4,5},{5,6},{6,7},{7,0},{8,9},{9,10},{10,1... | collective-permute-start | bytes 1572872 | tf_op jit(solution)/shard_map/ppermute | solution.py:16
  207.7 10.4 %collective-permute-start.1 = (bf16[128,2048]{1,0:T(8,128)(2,1)S(1)}, bf16[128,2048]{1,0:T(8,128)(2,1)S(1)}, u32[]{:S(2)}, u32[]{:S(2)}) collective-permute-start(bf16[128,2048]{1,0:T(8,128)(2,1)S(1)} %collective-permute-done), channel_id=1, source_target_pairs={{0,1},{1,2},{2,3},{3,4},{4,5},{5,6},{6,7},{7,0},{8,9},{9,10},{10,1... | collective-permute-start | bytes 1572872 | tf_op jit(solution)/shard_map/ppermute | solution.py:16
  218.1 20.8 %copy-start.3 = (bf16[128,2048]{1,0:T(8,128)(2,1)}, bf16[128,2048]{1,0:T(8,128)(2,1)S(1)}, u32[]{:S(2)}) copy-start(bf16[128,2048]{1,0:T(8,128)(2,1)S(1)} %collective-permute-done.1) | copy-start | bytes 1572868
  218.1 10.4 %collective-permute-start.2 = (bf16[128,2048]{1,0:T(8,128)(2,1)S(1)}, bf16[128,2048]{1,0:T(8,128)(2,1)S(1)}, u32[]{:S(2)}, u32[]{:S(2)}) collective-permute-start(bf16[128,2048]{1,0:T(8,128)(2,1)S(1)} %collective-permute-done.1), channel_id=1, source_target_pairs={{0,1},{1,2},{2,3},{3,4},{4,5},{5,6},{6,7},{7,0},{8,9},{9,10},{10,1... | collective-permute-start | bytes 1572872 | tf_op jit(solution)/shard_map/ppermute | solution.py:16
  228.5 10.4 %copy-start.4 = (bf16[128,2048]{1,0:T(8,128)(2,1)}, bf16[128,2048]{1,0:T(8,128)(2,1)S(1)}, u32[]{:S(2)}) copy-start(bf16[128,2048]{1,0:T(8,128)(2,1)S(1)} %collective-permute-done.2) | copy-start | bytes 1572868
  228.5 10.4 %collective-permute-start.3 = (bf16[128,2048]{1,0:T(8,128)(2,1)S(1)}, bf16[128,2048]{1,0:T(8,128)(2,1)S(1)}, u32[]{:S(2)}, u32[]{:S(2)}) collective-permute-start(bf16[128,2048]{1,0:T(8,128)(2,1)S(1)} %collective-permute-done.2), channel_id=1, source_target_pairs={{0,1},{1,2},{2,3},{3,4},{4,5},{5,6},{6,7},{7,0},{8,9},{9,10},{10,1... | collective-permute-start | bytes 1572872 | tf_op jit(solution)/shard_map/ppermute | solution.py:16
  238.9 10.5 %collective-permute-start.4 = (bf16[128,2048]{1,0:T(8,128)(2,1)S(1)}, bf16[128,2048]{1,0:T(8,128)(2,1)}, u32[]{:S(2)}, u32[]{:S(2)}) collective-permute-start(bf16[128,2048]{1,0:T(8,128)(2,1)S(1)} %collective-permute-done.3), channel_id=1, source_target_pairs={{0,1},{1,2},{2,3},{3,4},{4,5},{5,6},{6,7},{7,0},{8,9},{9,10},{10,1... | collective-permute-start | bytes 1572872 | tf_op jit(solution)/shard_map/ppermute | solution.py:16
  249.5 10.6 %collective-permute-start.5 = (bf16[128,2048]{1,0:T(8,128)(2,1)}, bf16[128,2048]{1,0:T(8,128)(2,1)S(1)}, u32[]{:S(2)}, u32[]{:S(2)}) collective-permute-start(bf16[128,2048]{1,0:T(8,128)(2,1)} %collective-permute-done.4), channel_id=1, source_target_pairs={{0,1},{1,2},{2,3},{3,4},{4,5},{5,6},{6,7},{7,0},{8,9},{9,10},{10,1... | collective-permute-start | bytes 1572872 | tf_op jit(solution)/shard_map/ppermute | solution.py:16
  260.1 10.4 %collective-permute-start.6 = (bf16[128,2048]{1,0:T(8,128)(2,1)S(1)}, bf16[128,2048]{1,0:T(8,128)(2,1)S(1)}, u32[]{:S(2)}, u32[]{:S(2)}) collective-permute-start(bf16[128,2048]{1,0:T(8,128)(2,1)S(1)} %collective-permute-done.5), channel_id=1, source_target_pairs={{0,1},{1,2},{2,3},{3,4},{4,5},{5,6},{6,7},{7,0},{8,9},{9,10},{10,1... | collective-permute-start | bytes 1572872 | tf_op jit(solution)/shard_map/ppermute | solution.py:16
  (4 other events, 7.5 us)
Sparse Core Ops, SparseCore 0:
  9.2 38.0 all-gather.3
  49.3 47.1 all-gather.5
  286.6 48.1 reduce-scatter.1
